TPU v7x, 128 devices: a whole 4x4x4 slice. The times are simulated.
128 devices in a mesh: child: 2 (over z_lo), row: 16 (over x, y), col: 4 (over z_hi, core).
Axes of the slice: x: 4, y: 4, z: 4 (z_hi: 2, z_lo: 2; z = z_hi * 2 + z_lo), core: 2. Of those that a mesh axis runs over, the one named last changes fastest.
Arguments:
- child_fronts: float32 [2, 4096, 4096], P('child', 'row', 'col'), as said below
- root_front: float32 [8192, 8192], P('col', ('child', 'row')), as said below
- block_maps: int32 [2, 24], replicated, may hold values from 0 to 63, as said below
Outputs:
- child_factor: float32 [2, 4096, 1024], P('child', 'row')
- root_factor: float32 [8192, 512], P('col')
- root_trailing: float32 [8192, 8192], P('col', ('child', 'row'))
Inputs may be any that keep to these rules, and one draw needn't show every extreme that they name: `block_maps`: row c lists 24 different root blocks in increasing order; block 0 appears in the first row and the last root block in the last row. `child_fronts`: each front is symmetric and positive definite. `root_front`: symmetric and positive definite.
All inputs are finite; a program needn't handle non-finite values.
Results may differ from a plain program's by a relative error of at most 0.0003.
Values may be sent and summed in bfloat16 or wider, within the bound.
No kernel may reach another device: no remote copies, remote signals or barrier semaphores. Data moves between devices by JAX's collectives and lax.ppermute only.
A program may use at most 128 MiB of HBM per device.

v0:
```python
import jax
import jax.numpy as jnp
from jax import lax
from jax.sharding import PartitionSpec as P

R = 8192
PANEL = 512
CPAN = 2
BLK = 128
PIV = 1024
NCB = 24


def from_root(block, axis, holder):
    block = jnp.where(lax.axis_index(axis) == holder, block, jnp.zeros_like(block))
    return lax.psum(block, axis)


def lookup(table, first_idx, second_idx):
    hits = (first_idx[..., None, None] == jnp.arange(table.shape[0], dtype=jnp.int32)[:, None]) & (
        second_idx[..., None, None] == jnp.arange(table.shape[1], dtype=jnp.int32)[None, :]
    )
    return jnp.sum(jnp.where(hits, table, 0), axis=(-2, -1))


def panel_step(local_tile, first_col, is_root):
    row_block, col_block = local_tile.shape
    if is_root:
        row_pos = lax.axis_index("col")
        col_pos = lax.axis_index(("child", "row"))
    else:
        row_pos = lax.axis_index("row")
        col_pos = lax.axis_index("col")
    panel_width = min(PANEL, col_block)
    offset = first_col % col_block if col_block >= PANEL else 0
    portion = lax.slice_in_dim(local_tile, offset, offset + panel_width, axis=1)
    arrived = []
    for member in range(max(PANEL // col_block, 1)):
        holder = first_col // col_block + member
        if is_root:
            arrived.append(from_root(portion, ("child", "row"), holder))
        else:
            arrived.append(from_root(portion, "col", holder))
    panel_rows = jnp.concatenate(arrived, axis=1)
    diag_width = min(PANEL, row_block)
    diag_offset = first_col % row_block if row_block >= PANEL else 0
    diag_portion = lax.slice_in_dim(panel_rows, diag_offset, diag_offset + diag_width, axis=0)
    diag_parts = []
    for member in range(max(PANEL // row_block, 1)):
        holder = first_col // row_block + member
        if is_root:
            diag_parts.append(from_root(diag_portion, "col", holder))
        else:
            diag_parts.append(from_root(diag_portion, "row", holder))
    diagonal = jnp.concatenate(diag_parts, axis=0)
    diag_factor = jnp.linalg.cholesky(diagonal)
    solved = lax.linalg.triangular_solve(
        diag_factor, panel_rows, left_side=False, lower=True, transpose_a=True
    )
    row_ids = row_pos * row_block + jnp.arange(row_block, dtype=jnp.int32)
    factor_rows = jnp.where(row_ids[:, None] >= first_col, solved, 0.0)
    update_rows = jnp.where(row_ids[:, None] >= first_col + PANEL, solved, 0.0).astype(jnp.bfloat16)
    if is_root:
        all_rows = lax.all_gather(update_rows, "col", axis=0, tiled=True)
    else:
        all_rows = lax.all_gather(update_rows, "row", axis=0, tiled=True)
    column_rows = lax.dynamic_slice_in_dim(all_rows, col_pos * col_block, col_block, 0)
    update = lax.dot_general(
        update_rows, column_rows, (((1,), (1,)), ((), ())), preferred_element_type=jnp.float32
    )
    return (local_tile - update, factor_rows)


def local(child_fronts, root_front, block_maps):
    local_tile = child_fronts[0]
    factors = []
    for panel_index in range(CPAN):
        local_tile, factor_rows = panel_step(local_tile, panel_index * PANEL, False)
        factors.append(factor_rows)
    child_factor = jnp.concatenate(factors, axis=1)[None]
    row_block, col_block = local_tile.shape
    child_pos = lax.axis_index("child")
    col_pos = lax.axis_index("col")
    row_count = lax.axis_size("row")
    group_count = lax.axis_size(("child", "row"))
    col_count = lax.axis_size("col")
    row_blocks = row_block // BLK
    root_blocks = R // BLK
    target_blocks = R // col_count // BLK
    width_out = R // group_count
    sources = jnp.arange(group_count, dtype=jnp.int32)
    front_blocks = (sources % row_count)[:, None] * row_blocks + jnp.arange(
        row_blocks, dtype=jnp.int32
    )[None, :]
    contrib_rows = front_blocks - PIV // BLK
    source_child = jnp.broadcast_to((sources // row_count)[:, None], contrib_rows.shape)
    row_targets = lookup(block_maps, source_child, contrib_rows)
    row_valid = contrib_rows >= 0
    block_ids = jnp.arange(root_blocks, dtype=jnp.int32)
    full_rows = lax.all_gather(local_tile, "col", axis=1, tiled=True)
    contrib = full_rows[:, PIV:].reshape(row_block, NCB, BLK)
    col_targets = lookup(
        block_maps, jnp.full((NCB,), child_pos, dtype=jnp.int32), jnp.arange(NCB, dtype=jnp.int32)
    )
    col_table = (col_targets[:, None] == block_ids[None, :]).astype(jnp.float32)
    placed = jnp.einsum("ray,am->rmy", contrib, col_table, precision=lax.Precision.HIGHEST).reshape(
        row_block, group_count, width_out
    )
    keep_rows = row_valid & (row_targets // target_blocks == col_pos)
    row_table = (
        keep_rows[:, :, None]
        & (
            (row_targets % target_blocks)[:, :, None]
            == jnp.arange(target_blocks, dtype=jnp.int32)[None, None, :]
        )
    ).astype(jnp.float32)
    received = lax.all_to_all(placed, ("child", "row"), split_axis=1, concat_axis=0, tiled=True)
    count_cols = received.shape[2]
    stacked = received.reshape(group_count, row_blocks, BLK, count_cols)
    summed = jnp.einsum("stq,stxn->qxn", row_table, stacked, precision=lax.Precision.HIGHEST)
    added = summed.reshape(target_blocks * BLK, count_cols)
    assembled = root_front + added
    panel_index = 0
    assembled, factor_rows = panel_step(assembled, panel_index * PANEL, True)
    return (child_factor, factor_rows, assembled)


def solution(mesh):
    return jax.shard_map(
        local,
        mesh=mesh,
        in_specs=(P("child", "row", "col"), P("col", ("child", "row")), P()),
        out_specs=(P("child", "row", None), P("col", None), P("col", ("child", "row"))),
        check_vma=False,
    )
```

profile of v0, /device:TPU:1, one launch (start us, length us, event | category | flops | bytes accessed | tf_op | source)
XLA Modules:
  0.0 1564.4 jit_solution(4274154260043947339)
XLA Ops:
  9.7 47.3 %all-reduce.11.cloned.1.call-done = f32[256,512]{0,1:T(8,128)} async-done(((f32[256,512]{0,1:T(8,128)}), f32[256,512]{0,1:T(8,128)}) %all-reduce.11.cloned.1.call-update) | async-done | bytes 524304 | tf_op jit(solution)/shard_map/psum | solution.py:16
  57.0 2.1 broadcast_select_fusion.4
  59.1 85.8 %all-reduce.21.cloned.1.call-done = (f32[256,512]{0,1:T(8,128)}, f32[256,512]{0,1:T(8,128)}) async-done(((f32[256,512]{0,1:T(8,128)}, f32[256,512]{0,1:T(8,128)}), (f32[256,512]{0,1:T(8,128)}, f32[256,512]{0,1:T(8,128)})) %all-reduce.21.cloned.1.call-update) | async-done | bytes 1048592 | tf_op jit(solution)/shard_map/psum | solution.py:16
  148.8 11.7 cholesky.374
  160.5 9.8 custom-call.34
  173.0 11.7 cholesky.393
  184.7 10.0 custom-call.35
  196.3 11.7 cholesky.414
  208.8 9.8 custom-call.36
  220.1 11.7 cholesky.431
  232.4 12.5 compare_reduce_fusion.10
  247.7 8.0 while.6
  255.7 39.3 %custom-call.37 = f32[4,128,128]{1,2,0:T(8,128)S(1)} custom-call(f32[4,128,128]{2,1,0:T(8,128)S(1)} %get-tuple-element.27), custom_call_target="InvertDiagBlocksLowerTriangular" | custom-call | tf_op jit(solution)/shard_map/triangular_solve/custom-call.3 | solution.py:57
  301.9 57.4 %all-gather.5.cloned.1.call-done = bf16[4096,512]{0,1:T(8,128)(2,1)} async-done(((bf16[256,512]{0,1:T(8,128)(2,1)}), bf16[4096,512]{0,1:T(8,128)(2,1)}) %all-gather.5.cloned.1.call-update) | async-done | bytes 4194320 | tf_op jit(solution)/shard_map/all_gather | solution.py:66
  362.0 43.1 %all-reduce.13.cloned.1.call-done = f32[256,512]{0,1:T(8,128)} async-done(((f32[256,512]{0,1:T(8,128)}), f32[256,512]{0,1:T(8,128)}) %all-reduce.13.cloned.1.call-update) | async-done | bytes 524304 | tf_op jit(solution)/shard_map/psum | solution.py:16
  405.1 2.1 broadcast_select_fusion.2
  407.9 85.2 %all-reduce.19.cloned.1.call-done = (f32[256,512]{0,1:T(8,128)}, f32[256,512]{0,1:T(8,128)}) async-done(((f32[256,512]{0,1:T(8,128)}, f32[256,512]{0,1:T(8,128)}), (f32[256,512]{0,1:T(8,128)}, f32[256,512]{0,1:T(8,128)})) %all-reduce.19.cloned.1.call-update) | async-done | bytes 1048592 | tf_op jit(solution)/shard_map/psum | solution.py:16
  496.8 11.7 cholesky.446
  508.7 9.8 custom-call.38
  521.0 11.7 cholesky.465
  534.1 10.2 custom-call.39
  545.9 11.7 cholesky.486
  558.3 9.8 custom-call.40
  569.5 11.7 cholesky.503
  584.8 8.0 while.7
  592.8 39.3 %custom-call.41 = f32[4,128,128]{1,2,0:T(8,128)S(1)} custom-call(f32[4,128,128]{2,1,0:T(8,128)S(1)} %get-tuple-element.28), custom_call_target="InvertDiagBlocksLowerTriangular" | custom-call | tf_op jit(solution)/shard_map/triangular_solve/custom-call.3 | solution.py:57
  639.6 57.4 %all-gather.7.cloned.1.call-done = bf16[4096,512]{0,1:T(8,128)(2,1)} async-done(((bf16[256,512]{0,1:T(8,128)(2,1)}), bf16[4096,512]{0,1:T(8,128)(2,1)}) %all-gather.7.cloned.1.call-update) | async-done | bytes 4194320 | tf_op jit(solution)/shard_map/all_gather | solution.py:66
  697.0 2.8 convolution_subtract_fusion.3
  700.1 39.3 %all-gather.9.cloned.1.call-done = f32[256,4096]{0,1:T(8,128)} async-done(((f32[256,1024]{0,1:T(8,128)}), f32[256,4096]{0,1:T(8,128)}) %all-gather.9.cloned.1.call-update) | async-done | bytes 4194320 | tf_op jit(solution)/shard_map/all_gather | solution.py:100
  741.3 2.4 copy.63
  743.7 8.6 convolution_bitcast_fusion
  752.3 9.8 reshape.207
  762.1 11.4 copy.64
  773.5 7.0 all-to-all-start
  783.2 115.7 %all-to-all-done = f32[256,32,256]{2,0,1:T(8,128)} async-done(((f32[256,32,256]{2,0,1:T(8,128)}), f32[256,32,256]{2,0,1:T(8,128)}, u32[]{:S(2)}, u32[]{:S(2)}) %all-to-all-start) | async-done | bytes 8388640 | tf_op jit(solution)/shard_map/all_to_all | solution.py:117
  898.9 10.5 copy.92
  909.4 5.2 fusion.97
  914.6 3.2 broadcast_select_fusion
  917.8 312.3 %all-reduce.17.cloned.1.call-done = (f32[2048,256]{0,1:T(8,128)}, f32[2048,256]{0,1:T(8,128)}) async-done(((f32[2048,256]{0,1:T(8,128)}, f32[2048,256]{0,1:T(8,128)}), (f32[2048,256]{0,1:T(8,128)}, f32[2048,256]{0,1:T(8,128)})) %all-reduce.17.cloned.1.call-update) | async-done | bytes 4194320 | tf_op jit(solution)/shard_map/psum | solution.py:16
  1230.1 2.3 fusion.13
  1232.5 68.1 %all-reduce.15.cloned.1.call-done = f32[512,512]{0,1:T(8,128)} async-done(((f32[512,512]{0,1:T(8,128)}), f32[512,512]{0,1:T(8,128)}) %all-reduce.15.cloned.1.call-update) | async-done | bytes 1048592 | tf_op jit(solution)/shard_map/psum | solution.py:16
  1304.6 11.7 cholesky.518
  1316.3 9.8 custom-call.42
  1328.7 11.7 cholesky.537
  1343.3 10.6 custom-call.43
  1360.7 13.2 cholesky.558
  1378.3 11.3 custom-call.44
  1392.7 13.2 cholesky.575
  1418.0 12.0 while.5
  1418.6 2.3 dynamic-slice.20
  1421.7 2.3 dynamic-slice.20
  1424.7 2.3 dynamic-slice.20
  1427.7 2.2 dynamic-slice.20
  1430.1 40.1 %custom-call.26 = f32[4,128,128]{1,2,0:T(8,128)} custom-call(f32[4,128,128]{2,1,0:T(8,128)S(1)} %get-tuple-element.20), custom_call_target="InvertDiagBlocksLowerTriangular" | custom-call | tf_op jit(solution)/shard_map/triangular_solve | solution.py:57
  1470.2 2.3 fusion.14
  1472.6 2.5 convolution_subtract_fusion.2
  1476.2 2.4 convolution_subtract_fusion.1
  1479.7 3.4 fusion.6
  1490.1 2.5 copy.81
  1492.7 4.5 fusion.9
  1497.1 5.8 copy.82
  1502.9 46.4 %all-gather.11.cloned.1.call-done = bf16[8192,512]{0,1:T(8,128)(2,1)} async-done(((bf16[2048,512]{0,1:T(8,128)(2,1)}), bf16[8192,512]{0,1:T(8,128)(2,1)}) %all-gather.11.cloned.1.call-update) | async-done | bytes 8388624 | tf_op jit(solution)/shard_map/all_gather | solution.py:64
  1549.3 5.0 convolution_subtract_fusion
  1554.3 2.9 copy.83
  (221 shorter events, 109.3 us)
Async XLA Ops:
  7.2 49.8 %all-reduce.11.cloned.1.call-start = ((), (), s32[]{:S(2)}) async-start(), calls=%async_computation.1 | async-start | bytes 1048576 | tf_op jit(solution)/shard_map/psum | solution.py:16
  9.6 135.3 %all-reduce.21.cloned.1.call-start = ((), (), s32[]{:S(2)}) async-start(), calls=%async_computation.10 | async-start | bytes 2097152 | tf_op jit(solution)/shard_map/psum | solution.py:16
  59.1 300.2 %all-gather.5.cloned.1.call-start = ((), (), s32[]{:S(2)}) async-start(), calls=%async_computation.2 | async-start | bytes 4456448 | tf_op jit(solution)/shard_map/all_gather | solution.py:66
  147.8 1.0 copy-start.8
  299.3 62.6 %copy-start.9 = (f32[256,128]{0,1:T(8,128)}, f32[256,128]{0,1:T(8,128)S(1)}, u32[]{:S(2)}) copy-start(f32[256,128]{0,1:T(8,128)S(1)} %fusion.81) | copy-start | bytes 393220
  301.0 0.8 copy-start.11
  301.8 103.3 %all-reduce.13.cloned.1.call-start = ((), (), s32[]{:S(2)}) async-start(), calls=%async_computation.3 | async-start | bytes 1048576 | tf_op jit(solution)/shard_map/psum | solution.py:16
  362.0 131.0 %all-reduce.19.cloned.1.call-start = ((), (), s32[]{:S(2)}) async-start(), calls=%async_computation.9 | async-start | bytes 2097152 | tf_op jit(solution)/shard_map/psum | solution.py:16
  407.3 289.8 %all-gather.7.cloned.1.call-start = ((), (), s32[]{:S(2)}) async-start(), calls=%async_computation.4 | async-start | bytes 4456448 | tf_op jit(solution)/shard_map/all_gather | solution.py:66
  495.8 1.0 copy-start.6
  584.6 54.2 %copy-start.17 = (pred[256]{0:T(512)(128)(4,1)S(1)}, pred[256]{0:T(512)(128)(4,1)}, u32[]{:S(2)}) copy-start(pred[256]{0:T(512)(128)(4,1)} %fusion.109) | copy-start | bytes 772
  634.8 3.3 copy-start.5
  636.4 1.7 copy-start.10
  636.5 63.5 %copy-start.16 = (s32[2,24]{1,0:T(2,128)S(1)}, s32[2,24]{1,0:T(2,128)}, u32[]{:S(2)}) copy-start(s32[2,24]{1,0:T(2,128)} %param.8) | copy-start | bytes 580
  638.2 0.6 copy-start.12
  639.6 99.8 %all-gather.9.cloned.1.call-start = ((), (), s32[]{:S(2)}) async-start(), calls=%async_computation.5 | async-start | bytes 5242880 | tf_op jit(solution)/shard_map/all_gather | solution.py:100
  739.4 1.9 slice-start
  773.5 125.4 %all-to-all-start = ((f32[256,32,256]{2,0,1:T(8,128)}), f32[256,32,256]{2,0,1:T(8,128)}, u32[]{:S(2)}, u32[]{:S(2)}) async-start(f32[256,32,256]{2,0,1:T(8,128)} %copy.64), calls=%async_computation | async-start | bytes 16777216 | tf_op jit(solution)/shard_map/all_to_all | solution.py:117
  780.6 449.5 %all-reduce.17.cloned.1.call-start = ((), (), s32[]{:S(2)}) async-start(), calls=%async_computation.8 | async-start | bytes 8388608 | tf_op jit(solution)/shard_map/psum | solution.py:16
  914.6 3.2 copy-start
  917.8 382.8 %all-reduce.15.cloned.1.call-start = ((), (), s32[]{:S(2)}) async-start(), calls=%async_computation.6 | async-start | bytes 2097152 | tf_op jit(solution)/shard_map/psum | solution.py:16
  1232.4 316.9 %all-gather.11.cloned.1.call-start = ((), (), s32[]{:S(2)}) async-start(), calls=%async_computation.7 | async-start | bytes 10485760 | tf_op jit(solution)/shard_map/all_gather | solution.py:64
  1303.6 1.0 copy-start.7
  1328.7 14.6 copy-start.13
  1359.4 0.7 copy-start.14
  1470.2 4.9 copy-start.15
  1472.6 3.6 copy-start.4
  1476.2 8.0 copy-start.1
  1479.7 4.5 copy-start.2
  1484.2 1.0 copy-start.3
Sparse Core Ops, SparseCore 0:
  11.1 45.8 all-reduce.10
  60.8 84.1 all-reduce.20
  301.9 57.2 all-gather.4
  362.2 42.9 all-reduce.12
  408.9 84.1 all-reduce.18
  639.7 57.2 all-gather.6
  700.0 39.3 all-gather.8
  917.9 312.1 all-reduce.16
  1233.2 67.3 all-reduce.14
  1487.1 62.1 all-gather.10
where the time goes:
time: 1580 us; the launch traced here: 1560 us
  waiting for transfers between devices  958 us (61%)
  other arithmetic  405 us (26%)
  local copies, waits for them, and re-layouts  101 us (6%)
  matrix products  68.5 us (4%)
  between operations  23.2 us (1%)
    psum x6, waiting for transfers between devices, from_root(): return lax.psum(block, axis)  642 us
    another operation x44, other arithmetic, panel_step(): diag_factor = jnp.linalg.cholesky(diagonal)  260 us
    another operation x7, other arithmetic, panel_step(): lax.linalg.triangular_solve(diag_factor, panel_rows, left_side=False, low...  120 us
    all_to_all x1, waiting for transfers between devices, local(): lax.all_to_all(placed, ('child', 'row'), split_axis=1, concat_axis=0, til...  116 us
    all_gather x2, waiting for transfers between devices, panel_step(): all_rows = lax.all_gather(update_rows, 'row', axis=0, tiled=True)  115 us
    all_gather x1, waiting for transfers between devices, panel_step(): all_rows = lax.all_gather(update_rows, 'col', axis=0, tiled=True)  46.4 us
    all_gather x1, waiting for transfers between devices, local(): full_rows = lax.all_gather(local_tile, 'col', axis=1, tiled=True)  39.3 us
  transfers between devices with their start and end apart: 11, of which 11 were waited for; matrix products, arithmetic and copies ran while one was open for 1% of the time, Pallas kernels for 0%

commit v1 on v0

v1 whole, which is shorter than its diff:
```python
import jax
import jax.numpy as jnp
from jax import lax
from jax.experimental import pallas as pl
from jax.experimental.pallas import tpu as pltpu
from jax.sharding import PartitionSpec as P

F32 = jnp.float32
BF16 = jnp.bfloat16
HI = lax.Precision.HIGHEST
ROWS, COLS = 16, 4
NCB = 24
VM = pltpu.CompilerParams(vmem_limit_bytes=56 << 20)


def lane_copy(v, k):
    return jnp.broadcast_to(v[:, k:k + 1], (8, 128))


def sub_copy(v, k):
    return jnp.broadcast_to(v[k:k + 1, :], (8, 128))


def dot(a, b, ca, cb):
    return lax.dot_general(a, b, (((ca,), (cb,)), ((), ())), precision=HI, preferred_element_type=F32)


def dot16(a, b, ca, cb):
    return lax.dot_general(a, b, (((ca,), (cb,)), ((), ())), preferred_element_type=F32)


def inverse_factor128(block):
    lane = lax.broadcasted_iota(jnp.int32, (8, 128), 1)
    sub = lax.broadcasted_iota(jnp.int32, (8, 128), 0)
    w = [block[8 * t:8 * t + 8, :] for t in range(16)]
    for s in range(16):
        c = {t: [lane_copy(w[t], 8 * s + j) for j in range(8)] for t in range(s, 16)}
        inside = (lane >= 8 * s) & (lane < 8 * s + 8)
        w[s] = jnp.where(inside, (lane - 8 * s == sub).astype(F32), w[s])
        for t in range(s + 1, 16):
            w[t] = jnp.where(inside, 0.0, w[t])
        for j in range(8):
            scale = lax.rsqrt(sub_copy(c[s][j], j))
            pivot_row = sub_copy(w[s], j) * scale
            ahead = {k: sub_copy(c[s][j], k) * scale for k in range(j + 1, 8)}
            for t in range(s, 16):
                l = c[t][j] * scale
                if t == s:
                    l = jnp.where(sub > j, l, 0.0)
                for k in range(j + 1, 8):
                    c[t][k] = c[t][k] - l * ahead[k]
                w[t] = w[t] - l * pivot_row
            w[s] = jnp.where(sub == j, pivot_row, w[s])
    return jnp.concatenate([jnp.where(lane <= sub + 8 * t, w[t], 0.0) for t in range(16)], axis=0)


def inverse_factor512(a, b):
    n = 512
    b[...] = jnp.zeros((n, n), F32)
    for k in range(n // 128):
        o = 128 * k
        g = inverse_factor128(a[o:o + 128, o:o + 128])
        if k > 0:
            b[o:o + 128, 0:o] = dot(g, b[o:o + 128, 0:o], 1, 0)
        b[o:o + 128, o:o + 128] = g
        r = o + 128
        if r < n:
            l = dot(a[r:n, o:o + 128], g, 1, 1)
            a[r:n, r:n] = a[r:n, r:n] - dot(l, l, 1, 1)
            b[r:n, 0:r] = b[r:n, 0:r] - dot(l, b[o:o + 128, 0:r], 1, 0)


def head_kernel(d_ref, inv_ref, a):
    for s in range(16):
        for h in range(2):
            a[256 * h + 16 * s:256 * h + 16 * s + 16, :] = d_ref[s, h]
    inverse_factor512(a, inv_ref)


def second_kernel(mask_ref, d_ref, inv0_ref, c_ref, p_ref, u_ref, d10, a, inv1):
    for s in range(16):
        for h in range(2):
            o = 256 * h + 16 * s
            d10[o:o + 16, :] = d_ref[s, h, :, 0:512]
            a[o:o + 16, :] = d_ref[s, h, :, 512:1024]
    inv0 = inv0_ref[...]
    u10 = dot(d10[...], inv0, 1, 1).astype(BF16)
    a[...] = a[...] - dot16(u10, u10, 1, 1)
    p0 = dot(c_ref[:, 0:512], inv0, 1, 1)
    u0 = p0.astype(BF16)
    c1 = c_ref[:, 512:1024] - dot16(u0, u10, 1, 1)
    inverse_factor512(a, inv1)
    p1 = dot(c1, inv1[...], 1, 1)
    p_ref[:, 0:512] = p0
    p_ref[:, 512:1024] = jnp.where(mask_ref[0] > 0, p1, 0.0)
    u_ref[:, 0:512] = u0
    u_ref[:, 512:1024] = p1.astype(BF16)


def place_kernel(bulk_ref, panel_ref, y_ref, o_ref, p_ref):
    def one(slot, carry):
        b = bulk_ref[slot]
        col = pl.multiple_of(jnp.maximum(b, 0) * 128, 128)
        v = y_ref[:, pl.ds(col, 128)]
        out = pl.multiple_of((slot % 4) * 128, 128)
        o_ref[slot // 4, :, pl.ds(out, 128)] = jnp.where(b >= 0, v, 0.0)
        return carry

    lax.fori_loop(0, 64, one, 0)
    for m in range(4):
        b = panel_ref[m]
        col = pl.multiple_of(jnp.maximum(b, 0) * 128, 128)
        p_ref[:, 128 * m:128 * m + 128] = jnp.where(b >= 0, y_ref[:, pl.ds(col, 128)], 0.0)


def select_kernel(idx_ref, u_ref, o_ref):
    for i in range(8):
        b = idx_ref[i]
        v = u_ref[jnp.maximum(b, 0) + 8]
        o_ref[i] = jnp.where(b >= 0, v, jnp.zeros_like(v))


def schur_kernel(rows_ref, panel_ref, u_ref, ucol_ref, f_ref, fp_ref, own_ref, other_ref, z_ref, t_ref):
    upan = jnp.concatenate([ucol_ref[q, 4 + m] for m in range(4) for q in range(4)], axis=0)
    ubulk = jnp.concatenate([ucol_ref[q, j] for j in range(4) for q in range(4)], axis=0)

    def picked(ref, i):
        b = ref[i]
        u = u_ref[jnp.maximum(b, 0) + 8]
        f = fp_ref[jnp.maximum(b, 0) + 8]
        return jnp.where(b >= 0, u, jnp.zeros_like(u)), jnp.where(b >= 0, f, 0.0)

    for ref, out in ((panel_ref, t_ref), (rows_ref, z_ref)):
        us, fs = zip(*[picked(ref, i) for i in range(4)])
        out[...] = jnp.concatenate(fs, axis=0) - dot16(jnp.concatenate(us, axis=0), upan, 1, 1)
    rows = u_ref[8:32].reshape(768, 1024)
    s = f_ref[8:32].reshape(768, 512) - dot16(rows, ubulk, 1, 1)
    own_ref[...] = s[:, 0:256]
    other_ref[...] = s[:, 256:512]


def root_kernel(t_ref, inv_ref, a):
    for q in range(4):
        for m in range(4):
            a[128 * m + 32 * q:128 * m + 32 * q + 32, :] = t_ref[q, m]
    inverse_factor512(a, inv_ref)


def spread_kernel(mine_ref, theirs_ref, own_ref, got_ref, o_ref):
    def one(m, carry):
        i = mine_ref[m]
        j = theirs_ref[m]
        v = own_ref[jnp.maximum(i, 0)]
        w = got_ref[jnp.maximum(j, 0)]
        o_ref[m] = jnp.where(i >= 0, v, 0.0) + jnp.where(j >= 0, w, 0.0)
        return carry

    lax.fori_loop(0, 64, one, 0)


def last_kernel(flag_ref, panel_ref, inv_ref, cp_ref, root_ref, got_ref, p_ref, o_ref, ug, cps):
    step = pl.program_id(0)

    @pl.when(step == 0)
    def _():
        for q in range(4):
            for m in range(4):
                cps[128 * m + 32 * q:128 * m + 32 * q + 32, :] = cp_ref[q, m]
        v = dot(inv_ref[...], cps[...], 1, 0).astype(BF16)
        ug[...] = jnp.where(flag_ref[0] > 0, v, jnp.zeros_like(v))

    p = dot(panel_ref[...], inv_ref[...], 1, 1)
    p_ref[...] = p
    u = p.astype(BF16)
    u = jnp.where((flag_ref[1] > 0) | (step >= 2), u, jnp.zeros_like(u))
    upd = dot16(u, ug[...], 1, 0)
    for m in range(2):
        for q in range(4):
            o = 128 * m + 32 * q
            o_ref[o:o + 32, :] = root_ref[o:o + 32, :] + got_ref[q, m] - upd[o:o + 32, :]


def vmem():
    return pl.BlockSpec(memory_space=pltpu.VMEM)


def smem():
    return pl.BlockSpec(memory_space=pltpu.SMEM)


def call(kernel, outs, n_scalar, n_vector, scratch=(), flops=0, name=None):
    return pl.pallas_call(
        kernel,
        out_shape=outs,
        in_specs=[smem()] * n_scalar + [vmem()] * n_vector,
        out_specs=jax.tree.map(lambda _: vmem(), outs),
        scratch_shapes=list(scratch),
        compiler_params=VM,
        cost_estimate=pl.CostEstimate(flops=flops, transcendentals=0, bytes_accessed=1 << 20),
        name=name,
    )


def sds(shape, dtype=F32):
    return jax.ShapeDtypeStruct(shape, dtype)


def exchange(x, axis):
    return lax.all_to_all(x, axis, split_axis=0, concat_axis=0, tiled=True)


def gather(x, axis, n):
    return exchange(jnp.broadcast_to(x[None], (n,) + x.shape), axis)


def from_first_col(x, q):
    got = lax.ppermute(x, "col", [(0, 2)])
    x = jnp.where(q == 2, got, x)
    got = lax.ppermute(x, "col", [(0, 1), (2, 3)])
    return jnp.where(q % 2 == 1, got, x)


def swap_child(x):
    return lax.ppermute(x, "child", [(0, 1), (1, 0)])


def local(child_fronts, root_front, block_maps):
    front = child_fronts[0]
    child = lax.axis_index("child")
    r = lax.axis_index("row")
    q = lax.axis_index("col")
    blocks = jnp.arange(64, dtype=jnp.int32)
    order = jnp.arange(1, NCB + 1, dtype=jnp.int32)
    inverse = jnp.sum(jnp.where(block_maps[:, :, None] == blocks, order[None, :, None], 0), axis=1) - 1
    mine = jnp.where(child == 0, inverse[0], inverse[1])
    theirs = jnp.where(child == 0, inverse[1], inverse[0])

    def pick(idx):
        return jnp.sum(jnp.where(idx[:, None] == blocks[None, :], mine[None, :], 0), axis=1)

    slot = jnp.arange(64, dtype=jnp.int32)
    half = jnp.where(slot % 4 >= 2, 1 - child, child)
    bulk_idx = pick(32 * half + 2 * (slot // 4) + slot % 2)
    panel_idx = mine[0:4]
    four = jnp.arange(4, dtype=jnp.int32)
    col_idx = jnp.concatenate([pick(32 * jnp.where(four >= 2, 1 - child, child) + 2 * r + four % 2), panel_idx])
    row_idx = pick(16 * four + r)

    first = exchange(front[:, 0:512].reshape(16, 16, 512), "row")[0:2]
    first = from_first_col(first, q)
    d00 = gather(first, "row", ROWS)
    second = exchange(front.reshape(16, 16, 1024), "row")[2:4]
    second = from_first_col(second, q)
    d1 = gather(second, "row", ROWS)

    y = exchange(front.reshape(2, 4, 32, 1024).transpose(1, 0, 2, 3), "col").reshape(4, 64, 1024)
    wide = jnp.concatenate([y[1], y[2], y[3]], axis=1)
    placed, placed_panel = call(place_kernel, (sds((16, 64, 512)), sds((64, 512))), 2, 1, name="place")(
        bulk_idx, panel_idx, wide)
    f_bulk = exchange(placed, "row").reshape(32, 32, 512)
    f_panel = gather(placed_panel, "row", ROWS).reshape(32, 32, 512)

    raw_rows = exchange(root_front.reshape(16, 128, 256), "row")[0:2]
    raw_rows = jnp.where(child == 0, jnp.concatenate([raw_rows[0], raw_rows[1]], axis=1), 0.0)
    top = root_front[0:512].reshape(4, 4, 32, 256).transpose(1, 0, 2, 3)
    top = exchange(top, "col")[0].reshape(128, 256)
    at_left = jnp.where((child == 0) & (r == 0), top, 0.0)
    at_right = jnp.where((child == 0) & (r == 1), top, 0.0)
    raw_diag = lax.psum(jnp.concatenate([at_left, at_right], axis=1), "row")

    inv0 = call(head_kernel, sds((512, 512)), 0, 1, [pltpu.VMEM((512, 512), F32)], 2 * 10**10, "head")(d00)
    below = (r >= 2).astype(jnp.int32)[None]
    p, u = call(
        second_kernel, (sds((64, 1024)), sds((64, 1024), BF16)), 1, 3,
        [pltpu.VMEM((512, 512), F32)] * 3, 3 * 10**10, "second")(below, d1, inv0, y[0])
    child_factor = gather(p.reshape(2, 32, 1024), "col", COLS).transpose(1, 0, 2, 3).reshape(1, 256, 1024)
    u_all = gather(u.reshape(2, 32, 1024), "row", ROWS).reshape(32, 32, 1024)
    u_sel = call(select_kernel, sds((8, 32, 1024), BF16), 1, 1, name="select")(col_idx, u_all)
    u_col = gather(u_sel, "col", COLS)
    own, other, z, t = call(
        schur_kernel, (sds((768, 256)), sds((768, 256)), sds((128, 512)), sds((128, 512))), 2, 4,
        flops=3 * 10**9, name="schur")(row_idx, panel_idx, u_all, u_col, f_bulk, f_panel)

    t = t + raw_diag
    t = t + swap_child(t)
    t_all = gather(t.reshape(4, 32, 512), "col", COLS)
    inv_root = call(root_kernel, sds((512, 512)), 0, 1, [pltpu.VMEM((512, 512), F32)], 2 * 10**10, "root")(t_all)

    z = exchange(z.reshape(4, 32, 512), "col").reshape(128, 512) + raw_rows
    z = z + swap_child(z)
    panel = gather(z, "row", ROWS).reshape(2048, 512)

    got = swap_child(other)
    spread = call(spread_kernel, sds((64, 32, 256)), 2, 2, name="spread")(
        mine, theirs, own.reshape(24, 32, 256), got.reshape(24, 32, 256))
    head_cols = top.reshape(4, 32, 256) + spread[0:4]
    head_cols = gather(head_cols, "col", COLS)
    arrived = exchange(spread.reshape(4, 16, 32, 256), "col")

    flags = jnp.stack([16 * child + r >= 2, q > 0]).astype(jnp.int32)
    root_factor, trailing = pl.pallas_call(
        last_kernel,
        out_shape=(sds((2048, 512)), sds((2048, 256))),
        grid=(8,),
        in_specs=[
            smem(),
            pl.BlockSpec((256, 512), lambda i: (i, 0)),
            pl.BlockSpec((512, 512), lambda i: (0, 0)),
            pl.BlockSpec((4, 4, 32, 256), lambda i: (0, 0, 0, 0)),
            pl.BlockSpec((256, 256), lambda i: (i, 0)),
            pl.BlockSpec((4, 2, 32, 256), lambda i: (0, i, 0, 0)),
        ],
        out_specs=(pl.BlockSpec((256, 512), lambda i: (i, 0)), pl.BlockSpec((256, 256), lambda i: (i, 0))),
        scratch_shapes=[pltpu.VMEM((512, 256), BF16), pltpu.VMEM((512, 256), F32)],
        compiler_params=VM,
        name="last",
    )(flags, panel, inv_root, head_cols, root_front, arrived)
    return (child_factor, root_factor, trailing)


def solution(mesh):
    return jax.shard_map(
        local,
        mesh=mesh,
        in_specs=(P("child", "row", "col"), P("col", ("child", "row")), P()),
        out_specs=(P("child", "row", None), P("col", None), P("col", ("child", "row"))),
        check_vma=False,
    )
```

time: 1580 us -> 583 us (0.37)
  the two profiles are of different devices: /device:TPU:1 before, /device:TPU:92 now
where the time goes in v1:
time: 583 us; the launch traced here: 579 us
  waiting for transfers between devices  238 us (41%)
  blocking collectives  108 us (19%)
  Pallas kernels  99.2 us (17%)
  starting transfers between devices  90.4 us (16%)
  local copies, waits for them, and re-layouts  21.1 us (4%)
  between operations  14.6 us (3%)
  other arithmetic  8.2 us (1%)
    all_to_all x12, waiting for transfers between devices, exchange(): return lax.all_to_all(x, axis, split_axis=0, concat_axis=0, tiled=True)  113 us
    all_to_all x5, blocking collectives, exchange(): return lax.all_to_all(x, axis, split_axis=0, concat_axis=0, tiled=True)  108 us
    all_to_all x12, starting transfers between devices, exchange(): return lax.all_to_all(x, axis, split_axis=0, concat_axis=0, tiled=True)  82.3 us
    psum x1, waiting for transfers between devices, local(): raw_diag = lax.psum(jnp.concatenate([at_left, at_right], axis=1), 'row')  80.3 us
    ppermute x3, waiting for transfers between devices, swap_child(): return lax.ppermute(x, 'child', [(0, 1), (1, 0)])  30.6 us
    pallas_call x1, Pallas kernels, local(): call(second_kernel, (sds((64, 1024)), sds((64, 1024), BF16)), 1, 3, [pltp...  25.4 us
    pallas_call x1, Pallas kernels, local(): call(head_kernel, sds((512, 512)), 0, 1, [pltpu.VMEM((512, 512), F32)], 2...  21.9 us
    pallas_call x1, Pallas kernels, local(): call(root_kernel, sds((512, 512)), 0, 1, [pltpu.VMEM((512, 512), F32)], 2...  21.9 us
  transfers between devices with their start and end apart: 20, of which 15 were waited for; matrix products, arithmetic and copies ran while one was open for 3% of the time, Pallas kernels for 15%

profile of v1, /device:TPU:92, one launch (start us, length us, event | category | flops | bytes accessed | tf_op | source)
XLA Modules:
  0.0 578.7 jit_solution(15281764027779453224)
XLA Ops:
  7.2 1.1 slice.70
  8.2 0.8 copy.20
  9.1 4.8 all-to-all-start.13
  13.9 1.9 slice.74
  15.7 5.3 all-to-all-done.13
  21.1 7.1 %all-to-all-start.2 = ((f32[16,16,512]{2,1,0:T(8,128)}), f32[16,16,512]{2,1,0:T(8,128)S(1)}, u32[]{:S(2)}, u32[]{:S(2)}) async-start(f32[16,16,512]{2,1,0:T(8,128)} %bitcast.3), calls=%async_computation.2 | async-start | bytes 1048576 | tf_op jit(solution)/shard_map/all_to_all | solution.py:209
  28.2 1.3 copy.19
  29.5 6.3 %all-to-all-done.2 = f32[16,16,512]{2,1,0:T(8,128)S(1)} async-done(((f32[16,16,512]{2,1,0:T(8,128)}), f32[16,16,512]{2,1,0:T(8,128)S(1)}, u32[]{:S(2)}, u32[]{:S(2)}) %all-to-all-start.2) | async-done | bytes 524320 | tf_op jit(solution)/shard_map/all_to_all | solution.py:209
  35.7 18.1 %all_to_all.85 = f32[4,2,32,1024]{3,2,1,0:T(8,128)S(1)} all-to-all(f32[4,2,32,1024]{3,2,1,0:T(8,128)S(1)} %bitcast.51), channel_id=1, replica_groups=mesh['child'=2,'row'=16,'col'=4] {'col'}, dimensions={0} | all-to-all | bytes 2097152 | tf_op jit(solution)/shard_map/all_to_all | solution.py:209
  53.8 7.6 %all-to-all-start = ((f32[16,16,1024]{2,1,0:T(8,128)}), f32[16,16,1024]{2,1,0:T(8,128)S(1)}, u32[]{:S(2)}, u32[]{:S(2)}) async-start(f32[16,16,1024]{2,1,0:T(8,128)} %bitcast.1), calls=%async_computation | async-start | bytes 2097152 | tf_op jit(solution)/shard_map/all_to_all | solution.py:209
  61.5 1.3 collective-permute-start.2
  62.8 6.4 %collective-permute-done.2 = f32[2,16,512]{2,1,0:T(8,128)S(1)} collective-permute-done((f32[2,16,512]{2,1,0:T(8,128)S(1)}, f32[2,16,512]{2,1,0:T(8,128)S(1)}, u32[]{:S(2)}, u32[]{:S(2)}) %collective-permute-start.2) | collective-permute-done | bytes 65568 | tf_op jit(solution)/shard_map/ppermute | solution.py:217
  69.1 1.3 collective-permute-start.3
  70.5 0.9 collective-permute-done.3
  71.3 4.2 all-to-all-done
  75.7 19.4 %all_to_all.86.d_ref = f32[16,2,16,512]{3,2,1,0:T(8,128)} all-to-all(f32[16,2,16,512]{3,2,1,0:T(8,128)S(1)} %broadcast_in_dim.144), channel_id=1, replica_groups=mesh['child'=2,'row'=16,'col'=4] {'row'}, dimensions={0} | all-to-all | bytes 2097152 | tf_op jit(solution)/shard_map/all_to_all | solution.py:209
  95.1 7.9 %all-to-all-start.11 = ((f32[16,128,256]{2,1,0:T(8,128)}), f32[16,128,256]{2,1,0:T(8,128)S(1)}, u32[]{:S(2)}, u32[]{:S(2)}) async-start(f32[16,128,256]{2,1,0:T(8,128)} %bitcast.23), calls=%async_computation.11 | async-start | bytes 4194304 | tf_op jit(solution)/shard_map/all_to_all | solution.py:209
  104.3 0.9 slice.73
  105.2 1.3 collective-permute-start
  107.3 6.3 %collective-permute-done = f32[2,16,1024]{2,1,0:T(8,128)S(1)} collective-permute-done((f32[2,16,1024]{2,1,0:T(8,128)S(1)}, f32[2,16,1024]{2,1,0:T(8,128)S(1)}, u32[]{:S(2)}, u32[]{:S(2)}) %collective-permute-start) | collective-permute-done | bytes 131104 | tf_op jit(solution)/shard_map/ppermute | solution.py:217
  113.6 0.9 broadcast_select_fusion
  114.5 1.3 collective-permute-start.1
  115.8 0.9 fusion.9
  116.8 10.5 %all-to-all-done.11 = f32[16,128,256]{2,1,0:T(8,128)S(1)} async-done(((f32[16,128,256]{2,1,0:T(8,128)}), f32[16,128,256]{2,1,0:T(8,128)S(1)}, u32[]{:S(2)}, u32[]{:S(2)}) %all-to-all-start.11) | async-done | bytes 2097184 | tf_op jit(solution)/shard_map/all_to_all | solution.py:209
  127.2 1.8 broadcast_in_dim.143
  129.2 8.0 %all-to-all-start.1 = ((f32[16,2,16,1024]{3,2,1,0:T(8,128)}), f32[16,2,16,1024]{3,2,1,0:T(8,128)}, u32[]{:S(2)}, u32[]{:S(2)}) async-start(f32[16,2,16,1024]{3,2,1,0:T(8,128)} %broadcast_in_dim.143), calls=%async_computation.1 | async-start | bytes 4194304 | tf_op jit(solution)/shard_map/all_to_all | solution.py:209
  137.2 0.9 pad_maximum_fusion.y_ref
  138.2 3.6 place.1
  141.8 21.9 %head.1.inv0_ref = f32[512,512]{1,0:T(8,128)} custom-call(f32[16,2,16,512]{3,2,1,0:T(8,128)} %all_to_all.86.d_ref), custom_call_target="tpu_custom_call" | custom-call | flops 20000000000 | bytes 1048576 | tf_op jit(solution)/shard_map/head/pallas_call | solution.py:271
  163.7 1.6 broadcast_in_dim.161
  165.3 7.2 %all-to-all-start.9 = ((f32[16,64,512]{2,1,0:T(8,128)}), f32[16,64,512]{2,1,0:T(8,128)S(1)}, u32[]{:S(2)}, u32[]{:S(2)}) async-start(f32[16,64,512]{2,1,0:T(8,128)} %broadcast_in_dim.161), calls=%async_computation.9 | async-start | bytes 4194304 | tf_op jit(solution)/shard_map/all_to_all | solution.py:209
  172.5 25.4 %second.1 = (f32[64,1024]{1,0:T(8,128)}, bf16[64,1024]{1,0:T(8,128)(2,1)}) custom-call(s32[1]{0:T(128)} %bitcast.mask_ref, f32[16,2,16,1024]{3,2,1,0:T(8,128)} %all-to-all-done.1.d_ref, f32[512,512]{1,0:T(8,128)} %head.1.inv0_ref, f32[64,1024]{1,0:T(8,128)} %bitcast.65), custom_call_target="tpu_custom_call" | custom-call | flops 30000001024 | bytes 1048576 | tf_op jit(solution)/shard_map/second/pallas_call | solution.py:273
  197.9 1.3 broadcast_in_dim.153
  199.2 27.9 %all_to_all.87 = bf16[16,2,32,1024]{3,2,1,0:T(8,128)(2,1)} all-to-all(bf16[16,2,32,1024]{3,2,1,0:T(8,128)(2,1)S(1)} %broadcast_in_dim.153), channel_id=1, replica_groups=mesh['child'=2,'row'=16,'col'=4] {'row'}, dimensions={0} | all-to-all | bytes 4194304 | tf_op jit(solution)/shard_map/all_to_all | solution.py:209
  227.1 7.8 %all-to-all-start.8 = ((f32[16,64,512]{2,1,0:T(8,128)}), f32[16,64,512]{2,1,0:T(8,128)S(1)}, u32[]{:S(2)}, u32[]{:S(2)}) async-start(f32[16,64,512]{2,1,0:T(8,128)} %get-tuple-element.15), calls=%async_computation.8 | async-start | bytes 4194304 | tf_op jit(solution)/shard_map/all_to_all | solution.py:209
  236.2 2.4 select.17
  238.6 18.6 %all-to-all-done.8 = f32[16,64,512]{2,1,0:T(8,128)S(1)} async-done(((f32[16,64,512]{2,1,0:T(8,128)}), f32[16,64,512]{2,1,0:T(8,128)S(1)}, u32[]{:S(2)}, u32[]{:S(2)}) %all-to-all-start.8) | async-done | bytes 2097184 | tf_op jit(solution)/shard_map/all_to_all | solution.py:209
  257.2 1.7 broadcast_in_dim.156
  258.9 28.9 %all_to_all.88.ucol_ref = bf16[4,8,32,1024]{3,2,1,0:T(8,128)(2,1)} all-to-all(bf16[4,8,32,1024]{3,2,1,0:T(8,128)(2,1)S(1)} %broadcast_in_dim.156), channel_id=1, replica_groups=mesh['child'=2,'row'=16,'col'=4] {'col'}, dimensions={0} | all-to-all | bytes 4194304 | tf_op jit(solution)/shard_map/all_to_all | solution.py:209
  287.8 1.1 broadcast_in_dim.146
  288.9 6.7 %all-to-all-start.5 = ((f32[4,2,32,1024]{3,2,1,0:T(8,128)}), f32[4,2,32,1024]{3,2,1,0:T(8,128)S(1)}, u32[]{:S(2)}, u32[]{:S(2)}) async-start(f32[4,2,32,1024]{3,2,1,0:T(8,128)} %broadcast_in_dim.146), calls=%async_computation.5 | async-start | bytes 2097152 | tf_op jit(solution)/shard_map/all_to_all | solution.py:209
  296.3 6.5 %schur.1 = (f32[768,256]{1,0:T(8,128)}, f32[768,256]{1,0:T(8,128)}, f32[128,512]{1,0:T(8,128)}, f32[128,512]{1,0:T(8,128)}) custom-call(s32[4]{0:T(128)} %get-tuple-element.24.rows_ref, s32[4]{0:T(128)} %slice_bitcast_fusion.2.panel_ref, bf16[32,32,1024]{2,1,0:T(8,128)(2,1)} %bitcast.50, bf16[4,8,32,1024]{3,2,1,0:T(8,128)(2,1)} %all_to_all.88.ucol_ref, ...), custom_call_target="tpu_custom_call" | custom-call | flops 3000000000 | bytes 1048576 | tf_op jit(solution)/shard_map/schur/pallas_call | solution.py:280
  302.8 80.3 %all-reduce.2.cloned.1.call-done = f32[128,512]{1,0:T(8,128)} async-done(((f32[128,512]{1,0:T(8,128)}), f32[128,512]{1,0:T(8,128)}) %all-reduce.2.cloned.1.call-update) | async-done | bytes 262160 | tf_op jit(solution)/shard_map/psum | solution.py:269
  383.1 1.1 add.122
  384.2 1.3 collective-permute-start.5
  386.3 4.8 all-to-all-start.10
  391.1 2.4 collective-permute-done.5
  393.6 16.6 %all-to-all-done.10 = f32[4,32,512]{2,1,0:T(8,128)S(1)} async-done(((f32[4,32,512]{2,1,0:T(8,128)}), f32[4,32,512]{2,1,0:T(8,128)S(1)}, u32[]{:S(2)}, u32[]{:S(2)}) %all-to-all-start.10) | async-done | bytes 262176 | tf_op jit(solution)/shard_map/all_to_all | solution.py:209
  410.2 1.1 broadcast_in_dim.166
  411.3 6.3 %all-to-all-start.14 = ((f32[4,4,32,512]{3,2,1,0:T(8,128)}), f32[4,4,32,512]{3,2,1,0:T(8,128)S(1)}, u32[]{:S(2)}, u32[]{:S(2)}) async-start(f32[4,4,32,512]{3,2,1,0:T(8,128)} %broadcast_in_dim.166), calls=%async_computation.14 | async-start | bytes 2097152 | tf_op jit(solution)/shard_map/all_to_all | solution.py:209
  417.6 3.6 spread.1
  421.3 0.9 slice_add_fusion
  422.2 8.2 %all-to-all-done.14.t_ref = f32[4,4,32,512]{3,2,1,0:T(8,128)S(1)} async-done(((f32[4,4,32,512]{3,2,1,0:T(8,128)}), f32[4,4,32,512]{3,2,1,0:T(8,128)S(1)}, u32[]{:S(2)}, u32[]{:S(2)}) %all-to-all-start.14) | async-done | bytes 1048608 | tf_op jit(solution)/shard_map/all_to_all | solution.py:209
  430.5 13.4 %all_to_all.89.cp_ref = f32[4,4,32,256]{3,2,1,0:T(8,128)} all-to-all(f32[4,4,32,256]{3,2,1,0:T(8,128)S(1)} %broadcast_in_dim.167), channel_id=1, replica_groups=mesh['child'=2,'row'=16,'col'=4] {'col'}, dimensions={0} | all-to-all | bytes 1048576 | tf_op jit(solution)/shard_map/all_to_all | solution.py:209
  443.9 6.8 %all-to-all-start.16 = ((f32[4,16,32,256]{3,2,1,0:T(8,128)}), f32[4,16,32,256]{3,2,1,0:T(8,128)S(1)}, u32[]{:S(2)}, u32[]{:S(2)}) async-start(f32[4,16,32,256]{3,2,1,0:T(8,128)} %bitcast.48), calls=%async_computation.16 | async-start | bytes 4194304 | tf_op jit(solution)/shard_map/all_to_all | solution.py:209
  450.7 1.0 slice_bitcast_fusion.1
  451.7 0.8 collective-permute-start.4
  452.5 28.2 %collective-permute-done.4 = f32[128,512]{1,0:T(8,128)S(1)} collective-permute-done((f32[128,512]{1,0:T(8,128)S(1)}, f32[128,512]{1,0:T(8,128)S(1)}, u32[]{:S(2)}, u32[]{:S(2)}) %collective-permute-start.4) | collective-permute-done | bytes 262176 | tf_op jit(solution)/shard_map/ppermute | solution.py:224
  480.8 2.7 broadcast_in_dim.163
  483.5 7.4 %all-to-all-start.12 = ((f32[16,128,512]{2,1,0:T(8,128)}), f32[16,128,512]{2,1,0:T(8,128)}, u32[]{:S(2)}, u32[]{:S(2)}) async-start(f32[16,128,512]{2,1,0:T(8,128)} %broadcast_in_dim.163), calls=%async_computation.12 | async-start | bytes 8388608 | tf_op jit(solution)/shard_map/all_to_all | solution.py:209
  491.5 1.0 copy.15
  492.5 21.9 %root.1.inv_ref = f32[512,512]{1,0:T(8,128)} custom-call(f32[4,4,32,512]{3,2,1,0:T(8,128)} %copy-done.7), custom_call_target="tpu_custom_call" | custom-call | flops 20000000000 | bytes 1048576 | tf_op jit(solution)/shard_map/root/pallas_call | solution.py:287
  514.4 43.3 %all-to-all-done.12 = f32[16,128,512]{2,1,0:T(8,128)} async-done(((f32[16,128,512]{2,1,0:T(8,128)}), f32[16,128,512]{2,1,0:T(8,128)}, u32[]{:S(2)}, u32[]{:S(2)}) %all-to-all-start.12) | async-done | bytes 4194336 | tf_op jit(solution)/shard_map/all_to_all | solution.py:209
  557.7 13.9 %last.1 = (f32[2048,512]{1,0:T(8,128)}, f32[2048,256]{1,0:T(8,128)}) custom-call(s32[2]{0:T(128)} %add_convert_fusion.flag_ref, f32[2048,512]{1,0:T(8,128)} %bitcast.26.panel_ref, f32[512,512]{1,0:T(8,128)} %root.1.inv_ref, f32[4,4,32,256]{3,2,1,0:T(8,128)} %all_to_all.89.cp_ref, f32[2048,256]{1,0:T(8,128)} %root_ref.1, f32[4,16,32,256]{3,2,1,0:T(8,128)} %copy-done), custom_call_target="tpu_custom_call" | custom-call | tf_op jit(solution)/shard_map/last/pallas_call | solution.py:301
  (62 shorter events, 6.2 us)
Async XLA Ops:
  9.1 12.0 %all-to-all-start.13 = ((f32[4,4,32,256]{3,2,1,0:T(8,128)}), f32[4,4,32,256]{3,2,1,0:T(8,128)S(1)}, u32[]{:S(2)}, u32[]{:S(2)}) async-start(f32[4,4,32,256]{3,2,1,0:T(8,128)} %bitcast.47), calls=%async_computation.13 | async-start | bytes 1048576 | tf_op jit(solution)/shard_map/all_to_all | solution.py:209
  21.1 14.7 %copy-start.5 = (f32[4,4,32,256]{3,2,1,0:T(8,128)}, f32[4,4,32,256]{3,2,1,0:T(8,128)S(1)}, u32[]{:S(2)}) copy-start(f32[4,4,32,256]{3,2,1,0:T(8,128)S(1)} %all-to-all-done.13) | copy-start | bytes 1572868
  21.1 14.7 %all-to-all-start.2 = ((f32[16,16,512]{2,1,0:T(8,128)}), f32[16,16,512]{2,1,0:T(8,128)S(1)}, u32[]{:S(2)}, u32[]{:S(2)}) async-start(f32[16,16,512]{2,1,0:T(8,128)} %bitcast.3), calls=%async_computation.2 | async-start | bytes 1048576 | tf_op jit(solution)/shard_map/all_to_all | solution.py:209
  53.8 21.8 %all-to-all-start = ((f32[16,16,1024]{2,1,0:T(8,128)}), f32[16,16,1024]{2,1,0:T(8,128)S(1)}, u32[]{:S(2)}, u32[]{:S(2)}) async-start(f32[16,16,1024]{2,1,0:T(8,128)} %bitcast.1), calls=%async_computation | async-start | bytes 2097152 | tf_op jit(solution)/shard_map/all_to_all | solution.py:209
  61.5 7.7 %collective-permute-start.2 = (f32[2,16,512]{2,1,0:T(8,128)S(1)}, f32[2,16,512]{2,1,0:T(8,128)S(1)}, u32[]{:S(2)}, u32[]{:S(2)}) collective-permute-start(f32[2,16,512]{2,1,0:T(8,128)S(1)} %slice.75), channel_id=1, source_target_pairs={{0,2},{4,6},{8,10},{12,14},{16,18},{20,22},{24,26},{28,30},{32,34}... | collective-permute-start | bytes 196616 | tf_op jit(solution)/shard_map/ppermute | solution.py:217
  69.1 2.2 collective-permute-start.3
  75.6 19.6 %copy-start.4 = (f32[16,16,1024]{2,1,0:T(8,128)}, f32[16,16,1024]{2,1,0:T(8,128)S(1)}, u32[]{:S(2)}) copy-start(f32[16,16,1024]{2,1,0:T(8,128)S(1)} %all-to-all-done) | copy-start | bytes 3145732
  95.1 7.9 %copy-start.13 = (s32[2,24]{1,0:T(2,128)S(1)}, s32[2,24]{1,0:T(2,128)}, u32[]{:S(2)}) copy-start(s32[2,24]{1,0:T(2,128)} %param.5) | copy-start | bytes 580
  95.1 32.1 %all-to-all-start.11 = ((f32[16,128,256]{2,1,0:T(8,128)}), f32[16,128,256]{2,1,0:T(8,128)S(1)}, u32[]{:S(2)}, u32[]{:S(2)}) async-start(f32[16,128,256]{2,1,0:T(8,128)} %bitcast.23), calls=%async_computation.11 | async-start | bytes 4194304 | tf_op jit(solution)/shard_map/all_to_all | solution.py:209
  103.7 131.1 %copy-start.12 = (s32[1,64]{1,0:T(1,128)}, s32[1,64]{1,0:T(1,128)S(1)}, u32[]{:S(2)}) copy-start(s32[1,64]{1,0:T(1,128)S(1)} %get-tuple-element.34) | copy-start | bytes 772
  105.2 8.4 %collective-permute-start = (f32[2,16,1024]{2,1,0:T(8,128)S(1)}, f32[2,16,1024]{2,1,0:T(8,128)S(1)}, u32[]{:S(2)}, u32[]{:S(2)}) collective-permute-start(f32[2,16,1024]{2,1,0:T(8,128)S(1)} %slice.73), channel_id=1, source_target_pairs={{0,2},{4,6},{8,10},{12,14},{16,18},{20,22},{24,26},{28,30},{32,34}... | collective-permute-start | bytes 393224 | tf_op jit(solution)/shard_map/ppermute | solution.py:217
  114.5 2.3 collective-permute-start.1
  127.2 2.0 copy-start.1
  129.0 8.2 %copy-start.8 = (f32[1,2,32,1024]{3,2,1,0:T(8,128)S(1)}, f32[1,2,32,1024]{3,2,1,0:T(8,128)}, u32[]{:S(2)}) copy-start(f32[1,2,32,1024]{3,2,1,0:T(8,128)} %get-tuple-element.28) | copy-start | bytes 786436
  129.0 8.2 %copy-start.9 = (f32[1,2,32,1024]{3,2,1,0:T(8,128)S(1)}, f32[1,2,32,1024]{3,2,1,0:T(8,128)}, u32[]{:S(2)}) copy-start(f32[1,2,32,1024]{3,2,1,0:T(8,128)} %get-tuple-element.29) | copy-start | bytes 786436
  129.2 34.5 %all-to-all-start.1 = ((f32[16,2,16,1024]{3,2,1,0:T(8,128)}), f32[16,2,16,1024]{3,2,1,0:T(8,128)}, u32[]{:S(2)}, u32[]{:S(2)}) async-start(f32[16,2,16,1024]{3,2,1,0:T(8,128)} %broadcast_in_dim.143), calls=%async_computation.1 | async-start | bytes 4194304 | tf_op jit(solution)/shard_map/all_to_all | solution.py:209
  141.8 22.0 %copy-start.11 = (f32[64,512]{1,0:T(8,128)S(1)}, f32[64,512]{1,0:T(8,128)}, u32[]{:S(2)}) copy-start(f32[64,512]{1,0:T(8,128)} %get-tuple-element.16) | copy-start | bytes 393220
  165.3 32.6 %all-to-all-start.9 = ((f32[16,64,512]{2,1,0:T(8,128)}), f32[16,64,512]{2,1,0:T(8,128)S(1)}, u32[]{:S(2)}, u32[]{:S(2)}) async-start(f32[16,64,512]{2,1,0:T(8,128)} %broadcast_in_dim.161), calls=%async_computation.9 | async-start | bytes 4194304 | tf_op jit(solution)/shard_map/all_to_all | solution.py:209
  197.9 29.2 %copy-start.2 = (f32[16,64,512]{2,1,0:T(8,128)}, f32[16,64,512]{2,1,0:T(8,128)S(1)}, u32[]{:S(2)}) copy-start(f32[16,64,512]{2,1,0:T(8,128)S(1)} %all-to-all-done.9) | copy-start | bytes 6291460
  227.1 8.5 %copy-start.14 = (s32[4]{0:T(128)S(1)}, s32[4]{0:T(128)}, u32[]{:S(2)}) copy-start(s32[4]{0:T(128)} %slice_bitcast_fusion.2.panel_ref) | copy-start | bytes 52
  227.1 30.2 %all-to-all-start.8 = ((f32[16,64,512]{2,1,0:T(8,128)}), f32[16,64,512]{2,1,0:T(8,128)S(1)}, u32[]{:S(2)}, u32[]{:S(2)}) async-start(f32[16,64,512]{2,1,0:T(8,128)} %get-tuple-element.15), calls=%async_computation.8 | async-start | bytes 4194304 | tf_op jit(solution)/shard_map/all_to_all | solution.py:209
  257.2 30.6 %copy-start.3 = (f32[16,64,512]{2,1,0:T(8,128)}, f32[16,64,512]{2,1,0:T(8,128)S(1)}, u32[]{:S(2)}) copy-start(f32[16,64,512]{2,1,0:T(8,128)S(1)} %all-to-all-done.8) | copy-start | bytes 6291460
  258.9 28.9 %copy-start.10 = (f32[64,1024]{1,0:T(8,128)S(1)}, f32[64,1024]{1,0:T(8,128)}, u32[]{:S(2)}) copy-start(f32[64,1024]{1,0:T(8,128)} %get-tuple-element.13) | copy-start | bytes 786436
  287.8 7.8 %copy-start.6 = (f32[4,4,32,256]{3,2,1,0:T(8,128)S(1)}, f32[4,4,32,256]{3,2,1,0:T(8,128)}, u32[]{:S(2)}) copy-start(f32[4,4,32,256]{3,2,1,0:T(8,128)} %copy-done.5) | copy-start | bytes 1572868
  288.9 97.4 %all-to-all-start.5 = ((f32[4,2,32,1024]{3,2,1,0:T(8,128)}), f32[4,2,32,1024]{3,2,1,0:T(8,128)S(1)}, u32[]{:S(2)}, u32[]{:S(2)}) async-start(f32[4,2,32,1024]{3,2,1,0:T(8,128)} %broadcast_in_dim.146), calls=%async_computation.5 | async-start | bytes 2097152 | tf_op jit(solution)/shard_map/all_to_all | solution.py:209
  295.5 87.6 %all-reduce.2.cloned.1.call-start = ((), (), s32[]{:S(2)}) async-start(), calls=%async_computation.17 | async-start | bytes 524288 | tf_op jit(solution)/shard_map/psum | solution.py:269
  384.2 9.3 %collective-permute-start.5 = (f32[128,512]{1,0:T(8,128)S(1)}, f32[128,512]{1,0:T(8,128)S(1)}, u32[]{:S(2)}, u32[]{:S(2)}) collective-permute-start(f32[128,512]{1,0:T(8,128)S(1)} %add.122), channel_id=1, source_target_pairs={{0,64},{64,0},{1,65},{65,1},{2,66},{66,2},{3,67},{67,3},{4,68},{68... | collective-permute-start | bytes 786440 | tf_op jit(solution)/shard_map/ppermute | solution.py:224
  385.5 32.1 %collective-permute-start.6 = (f32[768,256]{1,0:T(8,128)}, f32[768,256]{1,0:T(8,128)}, u32[]{:S(2)}, u32[]{:S(2)}) collective-permute-start(f32[768,256]{1,0:T(8,128)} %get-tuple-element.20), channel_id=1, source_target_pairs={{0,64},{64,0},{1,65},{65,1},{2,66},{66,2},{3,67},{67,3},{4,68},{68... | collective-permute-start | bytes 2359304 | tf_op jit(solution)/shard_map/ppermute | solution.py:224
  386.3 23.9 %all-to-all-start.10 = ((f32[4,32,512]{2,1,0:T(8,128)}), f32[4,32,512]{2,1,0:T(8,128)S(1)}, u32[]{:S(2)}, u32[]{:S(2)}) async-start(f32[4,32,512]{2,1,0:T(8,128)} %bitcast.64), calls=%async_computation.10 | async-start | bytes 524288 | tf_op jit(solution)/shard_map/all_to_all | solution.py:209
  411.3 19.1 %all-to-all-start.14 = ((f32[4,4,32,512]{3,2,1,0:T(8,128)}), f32[4,4,32,512]{3,2,1,0:T(8,128)S(1)}, u32[]{:S(2)}, u32[]{:S(2)}) async-start(f32[4,4,32,512]{3,2,1,0:T(8,128)} %broadcast_in_dim.166), calls=%async_computation.14 | async-start | bytes 2097152 | tf_op jit(solution)/shard_map/all_to_all | solution.py:209
  430.4 13.5 %copy-start.7 = (f32[4,4,32,512]{3,2,1,0:T(8,128)}, f32[4,4,32,512]{3,2,1,0:T(8,128)S(1)}, u32[]{:S(2)}) copy-start(f32[4,4,32,512]{3,2,1,0:T(8,128)S(1)} %all-to-all-done.14.t_ref) | copy-start | bytes 3145732
  443.9 36.9 %all-to-all-start.16 = ((f32[4,16,32,256]{3,2,1,0:T(8,128)}), f32[4,16,32,256]{3,2,1,0:T(8,128)S(1)}, u32[]{:S(2)}, u32[]{:S(2)}) async-start(f32[4,16,32,256]{3,2,1,0:T(8,128)} %bitcast.48), calls=%async_computation.16 | async-start | bytes 4194304 | tf_op jit(solution)/shard_map/all_to_all | solution.py:209
  451.7 29.0 %collective-permute-start.4 = (f32[128,512]{1,0:T(8,128)S(1)}, f32[128,512]{1,0:T(8,128)S(1)}, u32[]{:S(2)}, u32[]{:S(2)}) collective-permute-start(f32[128,512]{1,0:T(8,128)S(1)} %fusion), channel_id=1, source_target_pairs={{0,64},{64,0},{1,65},{65,1},{2,66},{66,2},{3,67},{67,3},{4,68},{68... | collective-permute-start | bytes 786440 | tf_op jit(solution)/shard_map/ppermute | solution.py:224
  480.8 2.7 copy-start
  483.5 74.3 %all-to-all-start.12 = ((f32[16,128,512]{2,1,0:T(8,128)}), f32[16,128,512]{2,1,0:T(8,128)}, u32[]{:S(2)}, u32[]{:S(2)}) async-start(f32[16,128,512]{2,1,0:T(8,128)} %broadcast_in_dim.163), calls=%async_computation.12 | async-start | bytes 8388608 | tf_op jit(solution)/shard_map/all_to_all | solution.py:209
Sparse Core Ops, SparseCore 0:
  299.5 83.5 all-reduce.1
